TPU v7x, 32 devices: a whole 2x2x4 slice. The times are simulated.
32 devices in a mesh: dp: 4 (over x, core), mp: 8 (over z, y).
Axes of the slice: x: 2, y: 2, z: 4, core: 2. Of those that a mesh axis runs over, the one named last changes fastest.
Arguments:
- tokens: bfloat16 [32768, 768], P(('dp', 'mp')), may hold values from -6 to 6
- lengths: int32 [64], P(('dp', 'mp')), may hold values from 16 to 512, as said below
- w_in: bfloat16 [768, 3072], P('dp', 'mp'), may hold values from -0.21875 to 0.21875
- b_in: bfloat16 [3072], P('mp'), may hold values from -3 to 3
- w_out: bfloat16 [3072, 768], P('mp', 'dp'), may hold values from -0.109375 to 0.109375
- b_out: float32 [768], replicated, may hold values from -2 to 2
- gain_mix: float32 [768], replicated, may hold values from 0.25 to 1.75
- shift_mix: float32 [768], replicated, may hold values from -2 to 2
- gain_ffn: float32 [768], replicated, may hold values from 0.25 to 1.75
- shift_ffn: float32 [768], replicated, may hold values from -2 to 2
- cotangent: bfloat16 [32768, 768], P(('dp', 'mp')), may hold values from -6 to 6
Outputs:
- layer_out: bfloat16 [32768, 768], P(('dp', 'mp'))
- grad_tokens: bfloat16 [32768, 768], P(('dp', 'mp'))
- grad_w_in: float32 [768, 3072], P('dp', 'mp')
- grad_b_in: float32 [3072], replicated
- grad_w_out: float32 [3072, 768], P('mp', 'dp')
- grad_b_out: float32 [768], replicated
- grad_gain_mix: float32 [768], replicated
- grad_shift_mix: float32 [768], replicated
- grad_gain_ffn: float32 [768], replicated
- grad_shift_ffn: float32 [768], replicated
Inputs may be any that keep to these rules, and one draw needn't show every extreme that they name: `lengths`: in every aligned block of 8 items exactly one has length 512; the others have at most 256.
All inputs are finite; a program needn't handle non-finite values.
Results may differ from a plain program's by a relative error of at most 0.0095.
Values may be sent and summed in bfloat16 or wider, within the bound.
No kernel may reach another device: no remote copies, remote signals or barrier semaphores. Data moves between devices by JAX's collectives and lax.ppermute only.
A program may use at most 320 MiB of HBM per device.

v0:
```python
from functools import partial
import math
import jax
import jax.numpy as jnp
from jax import lax
from jax.sharding import PartitionSpec as P

D = 768
FF = 3072
LEN = 512
MB = 2
SEQ_MB = 1
epsilon = 1e-06


def dft_tables(width):
    index = jnp.arange(width, dtype=jnp.int32)
    phase = index[:, None] * index[None, :] % width
    angle = phase.astype(jnp.float32) * (2.0 * math.pi / width)
    factor = 1.0 / math.sqrt(width)
    return (jnp.cos(angle) * factor, jnp.sin(angle) * factor)


def layer_norm(values, gain, shift):
    center = values - jnp.mean(values, axis=-1, keepdims=True)
    spread = jnp.mean(center * center, axis=-1, keepdims=True)
    return center * lax.rsqrt(spread + epsilon) * gain + shift


def masked_norm(values, gain, shift, live_mask):
    return live_mask * layer_norm(values, gain, shift)


def inner_rows(left, right):
    return lax.dot_general(
        left, right, (((1,), (1,)), ((), ())), preferred_element_type=jnp.float32
    )


def outer_rows(left, right):
    return lax.dot_general(
        left, right, (((0,), (0,)), ((), ())), preferred_element_type=jnp.float32
    )


def body(
    tokens, lengths, w_in, b_in, w_out, b_out, gain_mix, shift_mix, gain_ffn, shift_ffn, cotangent
):
    ff_local = w_in.shape[1]
    tok_rows = SEQ_MB * LEN
    cos_feat, sin_feat = dft_tables(D)
    feat_table = jnp.concatenate([cos_feat, sin_feat], axis=1).astype(jnp.bfloat16)
    cos_seq, sin_seq = dft_tables(LEN)
    seq_table = jnp.concatenate([cos_seq, -sin_seq], axis=1).astype(jnp.bfloat16)
    w_out_turned = w_out.T
    grad_w_in = jnp.zeros((D, ff_local), jnp.float32)
    grad_w_turned = jnp.zeros((D, ff_local), jnp.float32)
    grad_b_in = jnp.zeros((ff_local,), jnp.float32)
    grad_b_out = jnp.zeros((D,), jnp.float32)
    grad_gain_mix = jnp.zeros((D,), jnp.float32)
    grad_shift_mix = jnp.zeros((D,), jnp.float32)
    grad_gain_ffn = jnp.zeros((D,), jnp.float32)
    grad_shift_ffn = jnp.zeros((D,), jnp.float32)
    positions = jnp.arange(LEN, dtype=jnp.int32)
    outputs = []
    input_grads = []
    for micro in range(MB):
        inputs = lax.slice_in_dim(tokens, micro * tok_rows, (micro + 1) * tok_rows, axis=0)
        cot_part = lax.slice_in_dim(cotangent, micro * tok_rows, (micro + 1) * tok_rows, axis=0)
        item_lengths = lax.slice_in_dim(lengths, micro * SEQ_MB, (micro + 1) * SEQ_MB, axis=0)
        live_mask = (
            (positions[None, :] < item_lengths[:, None]).astype(jnp.float32).reshape(tok_rows, 1)
        )
        masked = inputs * live_mask.astype(jnp.bfloat16)
        spectra = jnp.dot(masked, feat_table, preferred_element_type=jnp.float32).astype(
            jnp.bfloat16
        )
        stacked = (
            spectra.reshape(SEQ_MB, LEN, 2, D).transpose(0, 2, 1, 3).reshape(SEQ_MB, 2 * LEN, D)
        )
        mixed = jnp.einsum(
            "st,gtd->gsd", seq_table, stacked, preferred_element_type=jnp.float32
        ).reshape(tok_rows, D)
        first, first_back = jax.vjp(
            layer_norm, masked.astype(jnp.float32) + mixed, gain_mix, shift_mix
        )
        first_low = first.astype(jnp.bfloat16)
        w_in_rows, w_out_rows = (
            lax.all_gather(w_in, "dp", axis=0, tiled=True),
            lax.all_gather(w_out_turned, "dp", axis=0, tiled=True),
        )
        gathered = lax.all_gather(first_low, "mp", axis=0, tiled=True)
        pre_act = jnp.dot(gathered, w_in_rows, preferred_element_type=jnp.float32) + b_in.astype(
            jnp.float32
        )
        activation, gelu_back = jax.vjp(jax.nn.gelu, pre_act)
        hidden = activation.astype(jnp.bfloat16)
        branch = (
            lax.psum_scatter(inner_rows(hidden, w_out_rows), "mp", scatter_dimension=0, tiled=True)
            + b_out
        )
        result, last_back = jax.vjp(
            partial(masked_norm, live_mask=live_mask), first + branch, gain_ffn, shift_ffn
        )
        outputs.append(result.astype(jnp.bfloat16))
        grad_second, gain_part, shift_part = last_back(cot_part.astype(jnp.float32))
        grad_gain_ffn = grad_gain_ffn + gain_part
        grad_shift_ffn = grad_shift_ffn + shift_part
        grad_branch = grad_second.astype(jnp.bfloat16)
        grad_b_out = grad_b_out + jnp.sum(grad_branch.astype(jnp.float32), axis=0)
        grad_gathered = lax.all_gather(grad_branch, "mp", axis=0, tiled=True)
        grad_hidden = jnp.dot(grad_gathered, w_out_rows, preferred_element_type=jnp.float32)
        grad_pre = gelu_back(grad_hidden)[0].astype(jnp.bfloat16)
        grad_b_in = grad_b_in + jnp.sum(grad_pre.astype(jnp.float32), axis=0)
        grad_w_in = grad_w_in + outer_rows(gathered, grad_pre)
        grad_w_turned = grad_w_turned + outer_rows(grad_gathered, hidden)
        grad_ffn = lax.psum_scatter(
            inner_rows(grad_pre, w_in_rows), "mp", scatter_dimension=0, tiled=True
        )
        grad_sum, gain_part, shift_part = first_back(grad_second + grad_ffn)
        grad_gain_mix = grad_gain_mix + gain_part
        grad_shift_mix = grad_shift_mix + shift_part
        grad_mixed = grad_sum.astype(jnp.bfloat16).reshape(SEQ_MB, LEN, D)
        grad_stack = jnp.einsum(
            "st,gsd->gtd", seq_table, grad_mixed, preferred_element_type=jnp.float32
        ).astype(jnp.bfloat16)
        grad_spectra = (
            grad_stack.reshape(SEQ_MB, 2, LEN, D).transpose(0, 2, 1, 3).reshape(tok_rows, 2 * D)
        )
        grad_masked = grad_sum + inner_rows(grad_spectra, feat_table)
        input_grads.append((grad_masked * live_mask).astype(jnp.bfloat16))
    offset = lax.axis_index("mp") * ff_local
    bias_grad_full = lax.dynamic_update_slice(jnp.zeros((FF,), jnp.float32), grad_b_in, (offset,))
    grad_w_in_part, grad_w_turned_part = (
        lax.psum_scatter(
            grad_w_in.astype(jnp.bfloat16), "dp", scatter_dimension=0, tiled=True
        ).astype(jnp.float32),
        lax.psum_scatter(
            grad_w_turned.astype(jnp.bfloat16), "dp", scatter_dimension=0, tiled=True
        ).astype(jnp.float32),
    )
    summed = lax.psum(
        (bias_grad_full, grad_b_out, grad_gain_mix, grad_shift_mix, grad_gain_ffn, grad_shift_ffn),
        ("dp", "mp"),
    )
    return (
        jnp.concatenate(outputs, axis=0),
        jnp.concatenate(input_grads, axis=0),
        grad_w_in_part,
        summed[0],
        grad_w_turned_part.T,
        summed[1],
        summed[2],
        summed[3],
        summed[4],
        summed[5],
    )


def solution(mesh):
    return jax.shard_map(
        body,
        mesh=mesh,
        in_specs=(
            P(("dp", "mp"), None),
            P(("dp", "mp")),
            P("dp", "mp"),
            P("mp"),
            P("mp", "dp"),
            P(),
            P(),
            P(),
            P(),
            P(),
            P(("dp", "mp"), None),
        ),
        out_specs=(
            P(("dp", "mp"), None),
            P(("dp", "mp"), None),
            P("dp", "mp"),
            P(),
            P("mp", "dp"),
            P(),
            P(),
            P(),
            P(),
            P(),
        ),
        check_vma=False,
    )
```

profile of v0, /device:TPU:0, one launch (start us, length us, event | category | flops | bytes accessed | tf_op | source)
XLA Modules:
  0.0 1429.6 jit_solution(16443774621906451339)
XLA Ops:
  7.2 5.4 negate_convert_fusion
  12.6 10.7 multiply_convert_fusion.2
  23.3 0.6 fusion.60
  23.9 0.6 fusion.46
  24.6 0.7 fusion.45
  25.4 1.2 copy.55
  26.8 0.9 copy-done.17
  27.7 3.0 convolution_convert_fusion
  31.4 0.9 copy-done.18
  32.6 1.0 fusion.61
  34.1 0.9 copy-done.11
  35.0 2.6 convolution_convert_fusion.1
  37.6 3.6 reshape.228
  41.5 0.9 copy-done.16
  42.7 1.0 fusion.62
  44.4 1.6 fusion.25
  46.1 0.7 all-gather.7.cloned.1.call-update
  47.0 9.4 all_gather.21
  56.4 8.2 all_gather.22
  64.7 83.8 %all-gather.5.cloned.1.call-done = bf16[4096,768]{0,1:T(8,128)(2,1)} async-done(((bf16[512,768]{0,1:T(8,128)(2,1)}), bf16[4096,768]{0,1:T(8,128)(2,1)}) %all-gather.5.cloned.1.call-update) | async-done | bytes 6291472 | tf_op jit(solution)/shard_map/all_gather | solution.py:92
  148.5 5.9 convolution_add_fusion.1
  154.3 2.7 copy-done.36
  157.1 6.6 fusion.51
  163.7 85.1 %all-gather.7.cloned.1.call-done = bf16[4096,768]{0,1:T(8,128)(2,1)} async-done(((bf16[512,768]{0,1:T(8,128)(2,1)}), bf16[4096,768]{0,1:T(8,128)(2,1)}) %all-gather.7.cloned.1.call-update) | async-done | bytes 6291472 | tf_op jit(solution)/shard_map/all_gather | solution.py:92
  248.8 5.9 convolution_add_fusion
  254.7 2.6 copy-done.37
  257.3 6.5 fusion.49
  263.8 2.6 fusion.58
  266.4 2.4 copy.58
  268.8 2.3 copy.57
  271.1 1.3 fusion.39
  272.4 186.1 %reduce-scatter.7.cloned.1.call-done = f32[512,768]{0,1:T(8,128)} async-done(((f32[4096,768]{0,1:T(8,128)}), f32[512,768]{0,1:T(8,128)}) %reduce-scatter.7.cloned.1.call-update) | async-done | bytes 1572880 | tf_op jit(solution)/shard_map/reduce_scatter | solution.py:99
  458.5 210.5 %reduce-scatter.9.cloned.1.call-done = f32[512,768]{0,1:T(8,128)} async-done(((f32[4096,768]{0,1:T(8,128)}), f32[512,768]{0,1:T(8,128)}) %reduce-scatter.9.cloned.1.call-update) | async-done | bytes 1572880 | tf_op jit(solution)/shard_map/reduce_scatter | solution.py:99
  668.9 2.8 fusion.57
  671.8 1.1 multiply_reduce_fusion.7
  672.9 0.8 multiply_reduce_fusion.1
  673.8 1.5 convert_reduce_fusion.3
  675.4 3.2 convert_reduce_fusion.2
  678.8 95.2 %all-gather.9.cloned.1.call-done = bf16[4096,768]{0,1:T(8,128)(2,1)} async-done(((bf16[512,768]{0,1:T(8,128)(2,1)}), bf16[4096,768]{0,1:T(8,128)(2,1)}) %all-gather.9.cloned.1.call-update) | async-done | bytes 6291472 | tf_op jit(solution)/shard_map/all_gather | solution.py:111
  774.0 11.4 convert_reduce_fusion.1
  785.4 88.2 %all-gather.11.cloned.1.call-done = bf16[4096,768]{0,1:T(8,128)(2,1)} async-done(((bf16[512,768]{0,1:T(8,128)(2,1)}), bf16[4096,768]{0,1:T(8,128)(2,1)}) %all-gather.11.cloned.1.call-update) | async-done | bytes 6291472 | tf_op jit(solution)/shard_map/all_gather | solution.py:111
  873.6 10.4 convert_reduce_fusion
  884.1 6.7 fusion.65
  890.7 6.5 fusion.23
  897.7 8.2 fusion.50
  905.9 9.0 fusion.24
  915.0 10.0 fusion.64
  925.2 10.1 fusion.63
  935.5 1.6 convert_element_type.192
  937.2 5.1 reduce-scatter.17.cloned.1.call-done
  942.2 1.6 convert_bitcast_fusion
  943.9 209.8 %reduce-scatter.13.cloned.1.call-done = f32[512,768]{0,1:T(8,128)} async-done(((f32[4096,768]{0,1:T(8,128)}), f32[512,768]{0,1:T(8,128)}) %reduce-scatter.13.cloned.1.call-update) | async-done | bytes 1572880 | tf_op jit(solution)/shard_map/reduce_scatter | solution.py:117
  1153.7 4.0 multiply_reduce_fusion.2
  1157.7 206.4 %reduce-scatter.11.cloned.1.call-done = f32[512,768]{0,1:T(8,128)} async-done(((f32[4096,768]{0,1:T(8,128)}), f32[512,768]{0,1:T(8,128)}) %reduce-scatter.11.cloned.1.call-update) | async-done | bytes 1572880 | tf_op jit(solution)/shard_map/reduce_scatter | solution.py:117
  1364.1 3.3 multiply_reduce_fusion.3
  1367.4 2.6 fusion.54
  1370.2 1.6 copy.47
  1371.8 2.7 convolution_convert_fusion.2
  1374.7 1.3 copy-done.10
  1376.3 1.4 multiply_convert_fusion.4
  1377.9 1.0 convolution_convert_fusion.3
  1379.1 1.4 multiply_convert_fusion.5
  1380.7 1.6 copy.48
  1382.3 40.3 %all-reduce = (f32[3072]{0:T(1024)}, f32[768]{0:T(1024)}, f32[768]{0:T(1024)}, f32[768]{0:T(1024)}, f32[768]{0:T(1024)}, /*index=5*/f32[768]{0:T(1024)}) all-reduce(f32[3072]{0:T(1024)S(1)} %add_dynamic-update-slice_fusion, f32[768]{0:T(1024)S(1)} %add.235, f32[768]{0:T(1024)S(1)} %add.236, ...), channel_id=1, replica_groups=mesh['dp'=4,'mp'=8] {'dp','mp'}, use_global_device_ids=true, to_apply=%region_23.24 | all-reduce | flops 6912 | bytes 55296 | tf_op jit(solution)/shard_map/psum | solution.py:142
  (122 shorter events, 5.9 us)
Async XLA Ops:
  7.2 16.2 %copy-start.34 = (s32[2]{0:T(128)S(1)}, s32[2]{0:T(128)}, u32[]{:S(2)}) copy-start(s32[2]{0:T(128)} %param.12) | copy-start | bytes 28
  7.2 18.1 %copy-start.8 = (bf16[1024,768]{1,0:T(8,128)(2,1)S(1)}, bf16[1024,768]{1,0:T(8,128)(2,1)}, u32[]{:S(2)}) copy-start(bf16[1024,768]{1,0:T(8,128)(2,1)} %param.11) | copy-start | bytes 4718596
  7.2 141.3 %all-gather.5.cloned.1.call-start = ((), (), s32[]{:S(2)}) async-start(), calls=%async_computation.6 | async-start | bytes 7077888 | tf_op jit(solution)/shard_map/all_gather | solution.py:92
  26.8 0.9 copy-start.17
  31.1 1.1 copy-start.18
  31.2 1.3 copy-start.21
  31.2 1.4 copy-start.24
  32.6 1.3 copy-start.13
  32.6 1.5 copy-start.15
  33.6 1.4 copy-start.11
  41.2 1.1 copy-start.16
  41.2 1.3 copy-start.22
  41.3 1.4 copy-start.25
  43.7 0.7 copy-start.30
  43.7 0.7 copy-start.32
  46.1 0.8 copy-start.35
  46.1 0.9 copy-start.28
  46.1 10.4 copy-start.29
  46.1 202.7 %all-gather.7.cloned.1.call-start = ((), (), s32[]{:S(2)}) async-start(), calls=%async_computation.8 | async-start | bytes 7077888 | tf_op jit(solution)/shard_map/all_gather | solution.py:92
  46.9 411.6 %reduce-scatter.7.cloned.1.call-start = ((), (), s32[]{:S(2)}) async-start(), calls=%async_computation.7 | async-start | bytes 14155776 | tf_op jit(solution)/shard_map/reduce_scatter | solution.py:99
  148.5 8.6 copy-start.19
  154.3 2.7 copy-start.36
  163.7 505.3 %reduce-scatter.9.cloned.1.call-start = ((), (), s32[]{:S(2)}) async-start(), calls=%async_computation.9 | async-start | bytes 14155776 | tf_op jit(solution)/shard_map/reduce_scatter | solution.py:99
  248.8 8.5 copy-start.20
  254.7 2.6 copy-start.37
  263.8 510.3 %all-gather.9.cloned.1.call-start = ((), (), s32[]{:S(2)}) async-start(), calls=%async_computation.10 | async-start | bytes 7077888 | tf_op jit(solution)/shard_map/all_gather | solution.py:111
  266.4 402.5 %copy-start.33 = (f32[768]{0:T(1024)S(1)}, f32[768]{0:T(1024)}, u32[]{:S(2)}) copy-start(f32[768]{0:T(1024)} %param.16) | copy-start | bytes 9220
  272.4 399.4 %copy-start.27 = (f32[768]{0:T(1024)S(1)}, f32[768]{0:T(1024)}, u32[]{:S(2)}) copy-start(f32[768]{0:T(1024)} %param.19) | copy-start | bytes 9220
  668.9 2.9 copy-start.2
  668.9 2.9 copy-start.3
  671.8 2.0 copy-start
  671.8 2.0 copy-start.1
  675.3 198.3 %all-gather.11.cloned.1.call-start = ((), (), s32[]{:S(2)}) async-start(), calls=%async_computation.12 | async-start | bytes 7077888 | tf_op jit(solution)/shard_map/all_gather | solution.py:111
  678.5 257.0 %reduce-scatter.15.cloned.1.call-start = ((), (), s32[]{:S(2)}) async-start(), calls=%async_computation.14 | async-start | bytes 737280 | tf_op jit(solution)/shard_map/reduce_scatter | solution.py:135
  873.6 10.4 copy-start.5
  884.0 6.7 copy-start.6
  897.2 45.0 %reduce-scatter.17.cloned.1.call-start = ((), (), s32[]{:S(2)}) async-start(), calls=%async_computation.15 | async-start | bytes 737280 | tf_op jit(solution)/shard_map/reduce_scatter | solution.py:138
  914.9 238.8 %reduce-scatter.13.cloned.1.call-start = ((), (), s32[]{:S(2)}) async-start(), calls=%async_computation.13 | async-start | bytes 14155776 | tf_op jit(solution)/shard_map/reduce_scatter | solution.py:117
  925.0 439.1 %reduce-scatter.11.cloned.1.call-start = ((), (), s32[]{:S(2)}) async-start(), calls=%async_computation.11 | async-start | bytes 14155776 | tf_op jit(solution)/shard_map/reduce_scatter | solution.py:117
  935.3 218.4 %copy-start.31 = (f32[768]{0:T(1024)S(1)}, f32[768]{0:T(1024)}, u32[]{:S(2)}) copy-start(f32[768]{0:T(1024)} %param.20) | copy-start | bytes 9220
  1364.1 3.3 copy-start.4
  1367.4 2.6 copy-start.7
  1371.8 2.9 copy-start.14
  1374.5 1.4 copy-start.10
  1374.5 1.7 copy-start.12
  1376.3 1.4 copy-start.9
  1376.3 1.5 copy-start.23
  1376.3 1.7 copy-start.26
Sparse Core Ops, SparseCore 0:
  46.2 102.1 all-gather.4
  151.1 97.6 all-gather.6
  252.4 206.0 reduce-scatter.6
  461.9 206.9 reduce-scatter.8
  675.4 98.5 all-gather.8
  775.9 97.6 all-gather.10
  897.3 20.2 reduce-scatter.14
  920.1 22.0 reduce-scatter.16
  945.8 207.8 reduce-scatter.12
  1157.1 206.9 reduce-scatter.10
where the time goes:
time: 1440 us; the launch traced here: 1430 us
  waiting for transfers between devices  1170 us (81%)
  matrix products  111 us (8%)
  blocking collectives  58 us (4%)
  other arithmetic  44 us (3%)
  local copies, waits for them, and re-layouts  29.4 us (2%)
  between operations  14.9 us (1%)
    reduce_scatter x2, waiting for transfers between devices, body(): lax.psum_scatter(inner_rows(grad_pre, w_in_rows), 'mp', scatter_dimension...  416 us
    reduce_scatter x2, waiting for transfers between devices, body(): lax.psum_scatter(inner_rows(hidden, w_out_rows), 'mp', scatter_dimension=...  397 us
    all_gather x2, waiting for transfers between devices, body(): grad_gathered = lax.all_gather(grad_branch, 'mp', axis=0, tiled=True)  183 us
    all_gather x2, waiting for transfers between devices, body(): gathered = lax.all_gather(first_low, 'mp', axis=0, tiled=True)  169 us
    psum x1, blocking collectives, body(): lax.psum((bias_grad_full, grad_b_out, grad_gain_mix, grad_shift_mix, grad...  40.3 us
    dot_general x6, matrix products, inner_rows(): lax.dot_general(left, right, (((1,), (1,)), ((), ())), preferred_element_...  35.9 us
    dot_general x4, matrix products, outer_rows(): lax.dot_general(left, right, (((0,), (0,)), ((), ())), preferred_element_...  30.3 us
  transfers between devices with their start and end apart: 10, of which 9 were waited for; matrix products, arithmetic and copies ran while one was open for 6% of the time, Pallas kernels for 0%

commit v1 on v0

--- a/solution.py
+++ b/solution.py
@@ -89,7 +89,15 @@
             lax.all_gather(w_in, "dp", axis=0, tiled=True),
             lax.all_gather(w_out_turned, "dp", axis=0, tiled=True),
         )
-        gathered = lax.all_gather(first_low, "mp", axis=0, tiled=True)
+        ways, here = (lax.axis_size("mp"), lax.axis_index("mp"))
+        grown, reach = (first_low, 1)
+        while reach < ways:
+            theirs = lax.ppermute(grown, "mp", [(d, d ^ reach) for d in range(ways)])
+            mine_first = jnp.concatenate([grown, theirs], axis=0)
+            theirs_first = jnp.concatenate([theirs, grown], axis=0)
+            grown = jnp.where(here & reach == 0, mine_first, theirs_first)
+            reach = 2 * reach
+        gathered = grown
         pre_act = jnp.dot(gathered, w_in_rows, preferred_element_type=jnp.float32) + b_in.astype(
             jnp.float32
         )

time: 1440 us -> 1590 us (1.10)
  waiting for transfers between devices: 1170 us -> 1300 us
    ppermute x0 -> x6, waiting for transfers between devices: none -> 496 us  [body(): theirs = lax.ppermute(grown, 'mp', [(d, d ^ reach) for d in range(ways)])]
    reduce_scatter x2, waiting for transfers between devices: 397 us -> 200 us  [body(): lax.psum_scatter(inner_rows(hidden, w_out_rows), 'mp', scatter_dimension=...]
    all_gather x2 -> x0, waiting for transfers between devices: 169 us -> none  [body(): gathered = lax.all_gather(first_low, 'mp', axis=0, tiled=True)]
  transfers between devices with their start and end apart: 10 -> 14, of which waited for: 9 -> 12; matrix products, arithmetic and copies ran while one was open for 6% -> 5% of each run, Pallas kernels for 0% -> 0%
where the time goes in v1:
time: 1590 us; the launch traced here: 1580 us
  waiting for transfers between devices  1300 us (82%)
  matrix products  111 us (7%)
  other arithmetic  56.3 us (4%)
  blocking collectives  55.8 us (4%)
  local copies, waits for them, and re-layouts  28.1 us (2%)
    ppermute x6, waiting for transfers between devices, body(): theirs = lax.ppermute(grown, 'mp', [(d, d ^ reach) for d in range(ways)])  496 us
    reduce_scatter x2, waiting for transfers between devices, body(): lax.psum_scatter(inner_rows(grad_pre, w_in_rows), 'mp', scatter_dimension...  416 us
    reduce_scatter x2, waiting for transfers between devices, body(): lax.psum_scatter(inner_rows(hidden, w_out_rows), 'mp', scatter_dimension=...  200 us
    all_gather x2, waiting for transfers between devices, body(): grad_gathered = lax.all_gather(grad_branch, 'mp', axis=0, tiled=True)  183 us
    psum x1, blocking collectives, body(): lax.psum((bias_grad_full, grad_b_out, grad_gain_mix, grad_shift_mix, grad...  40.3 us
    dot_general x6, matrix products, inner_rows(): lax.dot_general(left, right, (((1,), (1,)), ((), ())), preferred_element_...  35.9 us
  transfers between devices with their start and end apart: 14, of which 12 were waited for; matrix products, arithmetic and copies ran while one was open for 5% of the time, Pallas kernels for 0%

profile of v1, /device:TPU:0, one launch (start us, length us, event | category | flops | bytes accessed | tf_op | source)
XLA Modules:
  0.0 1577.1 jit_solution(5815085761014625078)
XLA Ops:
  7.2 5.4 negate_convert_fusion
  12.6 10.7 multiply_convert_fusion.2
  25.4 1.2 copy.55
  27.7 3.0 convolution_convert_fusion
  32.6 1.0 fusion.66
  34.4 2.6 convolution_convert_fusion.1
  37.0 3.6 reshape.228
  43.4 1.7 fusion.25
  45.1 3.0 collective-permute-start
  48.1 17.9 %collective-permute-done = bf16[512,768]{0,1:T(8,128)(2,1)} collective-permute-done((bf16[512,768]{0,1:T(8,128)(2,1)}, bf16[512,768]{0,1:T(8,128)(2,1)}, u32[]{:S(2)}, u32[]{:S(2)}) %collective-permute-start) | collective-permute-done | bytes 786464 | tf_op jit(solution)/shard_map/ppermute | solution.py:95
  65.9 3.7 maximum_select_fusion.4
  69.6 1.8 collective-permute-start.1
  71.4 34.1 %collective-permute-done.1 = bf16[1024,768]{0,1:T(8,128)(2,1)} collective-permute-done((bf16[1024,768]{0,1:T(8,128)(2,1)}, bf16[1024,768]{0,1:T(8,128)(2,1)}, u32[]{:S(2)}, u32[]{:S(2)}) %collective-permute-start.1) | collective-permute-done | bytes 1572896 | tf_op jit(solution)/shard_map/ppermute | solution.py:95
  105.5 5.5 maximum_select_fusion.2
  111.0 2.5 collective-permute-start.2
  113.5 7.5 all_gather.14
  121.1 8.0 all_gather.15
  129.0 119.0 %collective-permute-done.2 = bf16[2048,768]{0,1:T(8,128)(2,1)} collective-permute-done((bf16[2048,768]{0,1:T(8,128)(2,1)}, bf16[2048,768]{0,1:T(8,128)(2,1)}, u32[]{:S(2)}, u32[]{:S(2)}) %collective-permute-start.2) | collective-permute-done | bytes 3145760 | tf_op jit(solution)/shard_map/ppermute | solution.py:95
  248.0 8.5 convolution_add_fusion.1
  256.6 2.6 copy-done.46
  259.2 6.6 fusion.56
  265.8 1.2 collective-permute-start.3
  267.1 28.4 %collective-permute-done.3 = bf16[512,768]{0,1:T(8,128)(2,1)S(1)} collective-permute-done((bf16[512,768]{0,1:T(8,128)(2,1)}, bf16[512,768]{0,1:T(8,128)(2,1)S(1)}, u32[]{:S(2)}, u32[]{:S(2)}) %collective-permute-start.3) | collective-permute-done | bytes 786464 | tf_op jit(solution)/shard_map/ppermute | solution.py:95
  295.5 1.9 maximum_select_fusion.5
  297.5 108.5 %collective-permute-done.4 = bf16[1024,768]{0,1:T(8,128)(2,1)S(1)} collective-permute-done((bf16[1024,768]{0,1:T(8,128)(2,1)S(1)}, bf16[1024,768]{0,1:T(8,128)(2,1)S(1)}, u32[]{:S(2)}, u32[]{:S(2)}) %collective-permute-start.4) | collective-permute-done | bytes 1572896 | tf_op jit(solution)/shard_map/ppermute | solution.py:95
  406.1 1.2 maximum_select_fusion.3
  407.4 187.9 %collective-permute-done.5 = bf16[2048,768]{0,1:T(8,128)(2,1)S(1)} collective-permute-done((bf16[2048,768]{0,1:T(8,128)(2,1)S(1)}, bf16[2048,768]{0,1:T(8,128)(2,1)S(1)}, u32[]{:S(2)}, u32[]{:S(2)}) %collective-permute-start.5) | collective-permute-done | bytes 3145760 | tf_op jit(solution)/shard_map/ppermute | solution.py:95
  595.2 3.5 convolution_add_fusion
  598.8 2.6 copy-done.47
  601.4 6.5 fusion.54
  608.0 2.6 fusion.63
  610.6 2.3 copy.58
  612.9 2.3 copy.57
  615.2 1.3 fusion.40
  616.6 200.0 %reduce-scatter.9.cloned.1.call-done = f32[512,768]{0,1:T(8,128)} async-done(((f32[4096,768]{0,1:T(8,128)}), f32[512,768]{0,1:T(8,128)}) %reduce-scatter.9.cloned.1.call-update) | async-done | bytes 1572880 | tf_op jit(solution)/shard_map/reduce_scatter | solution.py:107
  816.6 2.8 fusion.62
  819.5 1.1 multiply_reduce_fusion.7
  821.5 1.5 convert_reduce_fusion.3
  823.2 3.1 convert_reduce_fusion.2
  826.4 95.3 %all-gather.3.cloned.1.call-done = bf16[4096,768]{0,1:T(8,128)(2,1)} async-done(((bf16[512,768]{0,1:T(8,128)(2,1)}), bf16[4096,768]{0,1:T(8,128)(2,1)}) %all-gather.3.cloned.1.call-update) | async-done | bytes 6291472 | tf_op jit(solution)/shard_map/all_gather | solution.py:119
  921.7 11.4 convert_reduce_fusion.1
  933.1 88.2 %all-gather.5.cloned.1.call-done = bf16[4096,768]{0,1:T(8,128)(2,1)} async-done(((bf16[512,768]{0,1:T(8,128)(2,1)}), bf16[4096,768]{0,1:T(8,128)(2,1)}) %all-gather.5.cloned.1.call-update) | async-done | bytes 6291472 | tf_op jit(solution)/shard_map/all_gather | solution.py:119
  1021.3 10.4 convert_reduce_fusion
  1031.8 3.8 fusion.27
  1035.6 9.5 fusion.23
  1045.3 8.2 fusion.55
  1053.6 9.0 fusion.24
  1062.7 9.9 fusion.68
  1073.0 10.1 fusion.69
  1083.3 1.6 convert_element_type.192
  1084.9 5.0 reduce-scatter.17.cloned.1.call-done
  1089.9 1.6 convert_bitcast_fusion
  1091.6 209.8 %reduce-scatter.11.cloned.1.call-done = f32[512,768]{0,1:T(8,128)} async-done(((f32[4096,768]{0,1:T(8,128)}), f32[512,768]{0,1:T(8,128)}) %reduce-scatter.11.cloned.1.call-update) | async-done | bytes 1572880 | tf_op jit(solution)/shard_map/reduce_scatter | solution.py:125
  1301.4 4.0 multiply_reduce_fusion.3
  1305.5 206.5 %reduce-scatter.13.cloned.1.call-done = f32[512,768]{0,1:T(8,128)} async-done(((f32[4096,768]{0,1:T(8,128)}), f32[512,768]{0,1:T(8,128)}) %reduce-scatter.13.cloned.1.call-update) | async-done | bytes 1572880 | tf_op jit(solution)/shard_map/reduce_scatter | solution.py:125
  1512.0 3.3 multiply_reduce_fusion.2
  1515.4 2.6 fusion.59
  1518.1 1.6 copy.47
  1519.7 2.2 convolution_convert_fusion.2
  1522.0 1.1 copy-done.16
  1523.5 1.4 multiply_convert_fusion.4
  1526.3 1.4 multiply_convert_fusion.5
  1527.9 1.6 copy.48
  1529.5 40.3 %all-reduce = (f32[3072]{0:T(1024)}, f32[768]{0:T(1024)}, f32[768]{0:T(1024)}, f32[768]{0:T(1024)}, f32[768]{0:T(1024)}, /*index=5*/f32[768]{0:T(1024)}) all-reduce(f32[3072]{0:T(1024)S(1)} %add_dynamic-update-slice_fusion, f32[768]{0:T(1024)S(1)} %add.235, f32[768]{0:T(1024)S(1)} %add.236, ...), channel_id=1, replica_groups=mesh['dp'=4,'mp'=8] {'dp','mp'}, use_global_device_ids=true, to_apply=%region_23.24 | all-reduce | flops 6912 | bytes 55296 | tf_op jit(solution)/shard_map/psum | solution.py:150
  (152 shorter events, 13.1 us)
Async XLA Ops:
  7.2 16.2 %copy-start.42 = (s32[2]{0:T(128)S(1)}, s32[2]{0:T(128)}, u32[]{:S(2)}) copy-start(s32[2]{0:T(128)} %param.12) | copy-start | bytes 28
  7.2 18.1 %copy-start.12 = (bf16[1024,768]{1,0:T(8,128)(2,1)S(1)}, bf16[1024,768]{1,0:T(8,128)(2,1)}, u32[]{:S(2)}) copy-start(bf16[1024,768]{1,0:T(8,128)(2,1)} %param.11) | copy-start | bytes 4718596
  7.2 609.4 %reduce-scatter.7.cloned.1.call-start = ((), (), s32[]{:S(2)}) async-start(), calls=%async_computation.6 | async-start | bytes 14155776 | tf_op jit(solution)/shard_map/reduce_scatter | solution.py:107
  26.8 0.9 copy-start.21
  31.1 1.1 copy-start.22
  31.2 1.3 copy-start.25
  31.2 1.4 copy-start.28
  32.6 1.3 copy-start.15
  32.6 1.6 copy-start.17
  32.6 1.8 copy-start.19
  33.9 3.1 copy-start.35
  40.6 1.1 copy-start.20
  40.7 1.3 copy-start.26
  40.7 1.4 copy-start.29
  42.1 1.3 copy-start.34
  42.1 1.3 copy-start.40
  43.4 1.7 copy-start.37
  45.1 20.8 %collective-permute-start = (bf16[512,768]{0,1:T(8,128)(2,1)}, bf16[512,768]{0,1:T(8,128)(2,1)}, u32[]{:S(2)}, u32[]{:S(2)}) collective-permute-start(bf16[512,768]{0,1:T(8,128)(2,1)} %get-tuple-element.81), channel_id=1, source_target_pairs={{0,1},{1,0},{2,3},{3,2},{4,5},{5,4},{6,7},{7,6},{8,9},{9,8},{10,11... | collective-permute-start | bytes 2359304 | tf_op jit(solution)/shard_map/ppermute | solution.py:95
  69.6 35.9 %collective-permute-start.1 = (bf16[1024,768]{0,1:T(8,128)(2,1)}, bf16[1024,768]{0,1:T(8,128)(2,1)}, u32[]{:S(2)}, u32[]{:S(2)}) collective-permute-start(bf16[1024,768]{0,1:T(8,128)(2,1)} %maximum_select_fusion.4), channel_id=1, source_target_pairs={{0,2},{1,3},{2,0},{3,1},{4,6},{5,7},{6,4},{7,5},{8,10},{9,11},{10,... | collective-permute-start | bytes 4718600 | tf_op jit(solution)/shard_map/ppermute | solution.py:95
  71.4 42.1 %copy-start.43 = (bf16[384]{0:T(512)(128)(2,1)S(1)}, bf16[384]{0:T(512)(128)(2,1)}, u32[]{:S(2)}) copy-start(bf16[384]{0:T(512)(128)(2,1)} %param.14) | copy-start | bytes 2308
  71.4 42.1 %copy-start.32 = (bf16[192,384]{1,0:T(8,128)(2,1)S(1)}, bf16[192,384]{1,0:T(8,128)(2,1)}, u32[]{:S(2)}) copy-start(bf16[192,384]{1,0:T(8,128)(2,1)} %param.13) | copy-start | bytes 442372
  71.4 49.6 %copy-start.33 = (bf16[384,192]{0,1:T(8,128)(2,1)S(1)}, bf16[384,192]{0,1:T(8,128)(2,1)}, u32[]{:S(2)}) copy-start(bf16[384,192]{0,1:T(8,128)(2,1)} %param.15) | copy-start | bytes 442372
  111.0 137.0 %collective-permute-start.2 = (bf16[2048,768]{0,1:T(8,128)(2,1)}, bf16[2048,768]{0,1:T(8,128)(2,1)}, u32[]{:S(2)}, u32[]{:S(2)}) collective-permute-start(bf16[2048,768]{0,1:T(8,128)(2,1)} %maximum_select_fusion.2), channel_id=1, source_target_pairs={{0,4},{1,5},{2,6},{3,7},{4,0},{5,1},{6,2},{7,3},{8,12},{9,13},{10,... | collective-permute-start | bytes 9437192 | tf_op jit(solution)/shard_map/ppermute | solution.py:95
  121.1 135.5 %copy-start.7 = (bf16[768,384]{1,0:T(8,128)(2,1)}, bf16[768,384]{1,0:T(8,128)(2,1)S(1)}, u32[]{:S(2)}) copy-start(bf16[768,384]{1,0:T(8,128)(2,1)S(1)} %all_gather.14) | copy-start | bytes 1769476
  129.0 127.5 %copy-start.23 = (bf16[768,384]{1,0:T(8,128)(2,1)}, bf16[768,384]{1,0:T(8,128)(2,1)S(1)}, u32[]{:S(2)}) copy-start(bf16[768,384]{1,0:T(8,128)(2,1)S(1)} %all_gather.15) | copy-start | bytes 1769476
  256.5 2.6 copy-start.46
  265.8 550.8 %reduce-scatter.9.cloned.1.call-start = ((), (), s32[]{:S(2)}) async-start(), calls=%async_computation.7 | async-start | bytes 14155776 | tf_op jit(solution)/shard_map/reduce_scatter | solution.py:107
  265.8 29.7 %collective-permute-start.3 = (bf16[512,768]{0,1:T(8,128)(2,1)}, bf16[512,768]{0,1:T(8,128)(2,1)S(1)}, u32[]{:S(2)}, u32[]{:S(2)}) collective-permute-start(bf16[512,768]{0,1:T(8,128)(2,1)} %get-tuple-element.82), channel_id=1, source_target_pairs={{0,1},{1,0},{2,3},{3,2},{4,5},{5,4},{6,7},{7,6},{8,9},{9,8},{10,11... | collective-permute-start | bytes 2359304 | tf_op jit(solution)/shard_map/ppermute | solution.py:95
  297.4 297.8 %copy-start.8 = (bf16[768,384]{1,0:T(8,128)(2,1)S(1)}, bf16[768,384]{1,0:T(8,128)(2,1)}, u32[]{:S(2)}) copy-start(bf16[768,384]{1,0:T(8,128)(2,1)} %copy-done.7) | copy-start | bytes 1769476
  297.4 108.7 %collective-permute-start.4 = (bf16[1024,768]{0,1:T(8,128)(2,1)S(1)}, bf16[1024,768]{0,1:T(8,128)(2,1)S(1)}, u32[]{:S(2)}, u32[]{:S(2)}) collective-permute-start(bf16[1024,768]{0,1:T(8,128)(2,1)S(1)} %maximum_select_fusion.5), channel_id=1, source_target_pairs={{0,2},{1,3},{2,0},{3,1},{4,6},{5,7},{6,4},{7,5},{8,10},{9,11},{10,... | collective-permute-start | bytes 4718600 | tf_op jit(solution)/shard_map/ppermute | solution.py:95
  407.3 191.5 %copy-start.9 = (bf16[2048,768]{0,1:T(8,128)(2,1)}, bf16[2048,768]{0,1:T(8,128)(2,1)S(1)}, u32[]{:S(2)}) copy-start(bf16[2048,768]{0,1:T(8,128)(2,1)S(1)} %maximum_select_fusion.3) | copy-start | bytes 9437188
  407.3 194.1 %copy-start.24 = (bf16[768,384]{1,0:T(8,128)(2,1)S(1)}, bf16[768,384]{1,0:T(8,128)(2,1)}, u32[]{:S(2)}) copy-start(bf16[768,384]{1,0:T(8,128)(2,1)} %copy-done.23) | copy-start | bytes 1769476
  407.3 187.9 %collective-permute-start.5 = (bf16[2048,768]{0,1:T(8,128)(2,1)S(1)}, bf16[2048,768]{0,1:T(8,128)(2,1)S(1)}, u32[]{:S(2)}, u32[]{:S(2)}) collective-permute-start(bf16[2048,768]{0,1:T(8,128)(2,1)S(1)} %maximum_select_fusion.3), channel_id=1, source_target_pairs={{0,4},{1,5},{2,6},{3,7},{4,0},{5,1},{6,2},{7,3},{8,12},{9,13},{10,... | collective-permute-start | bytes 9437192 | tf_op jit(solution)/shard_map/ppermute | solution.py:95
  595.2 3.6 copy-start.44
  598.8 2.6 copy-start.47
  607.9 313.8 %all-gather.3.cloned.1.call-start = ((), (), s32[]{:S(2)}) async-start(), calls=%async_computation.8 | async-start | bytes 7077888 | tf_op jit(solution)/shard_map/all_gather | solution.py:119
  610.6 206.0 %copy-start.41 = (f32[768]{0:T(1024)S(1)}, f32[768]{0:T(1024)}, u32[]{:S(2)}) copy-start(f32[768]{0:T(1024)} %param.16) | copy-start | bytes 9220
  616.6 203.0 %copy-start.31 = (f32[768]{0:T(1024)S(1)}, f32[768]{0:T(1024)}, u32[]{:S(2)}) copy-start(f32[768]{0:T(1024)} %param.19) | copy-start | bytes 9220
  816.6 2.9 copy-start.2
  816.6 2.9 copy-start.3
  819.5 2.0 copy-start
  819.5 2.0 copy-start.1
  823.0 198.3 %all-gather.5.cloned.1.call-start = ((), (), s32[]{:S(2)}) async-start(), calls=%async_computation.10 | async-start | bytes 7077888 | tf_op jit(solution)/shard_map/all_gather | solution.py:119
  826.4 256.9 %reduce-scatter.15.cloned.1.call-start = ((), (), s32[]{:S(2)}) async-start(), calls=%async_computation.12 | async-start | bytes 737280 | tf_op jit(solution)/shard_map/reduce_scatter | solution.py:143
  1021.3 10.4 copy-start.10
  1021.3 10.4 copy-start.45
  1031.7 3.8 copy-start.5
  1031.8 3.8 copy-start.6
  1045.1 44.8 %reduce-scatter.17.cloned.1.call-start = ((), (), s32[]{:S(2)}) async-start(), calls=%async_computation.13 | async-start | bytes 737280 | tf_op jit(solution)/shard_map/reduce_scatter | solution.py:146
  1062.6 238.8 %reduce-scatter.11.cloned.1.call-start = ((), (), s32[]{:S(2)}) async-start(), calls=%async_computation.9 | async-start | bytes 14155776 | tf_op jit(solution)/shard_map/reduce_scatter | solution.py:125
  1072.7 439.3 %reduce-scatter.13.cloned.1.call-start = ((), (), s32[]{:S(2)}) async-start(), calls=%async_computation.11 | async-start | bytes 14155776 | tf_op jit(solution)/shard_map/reduce_scatter | solution.py:125
  1083.1 218.4 %copy-start.39 = (f32[768]{0:T(1024)S(1)}, f32[768]{0:T(1024)}, u32[]{:S(2)}) copy-start(f32[768]{0:T(1024)} %param.20) | copy-start | bytes 9220
  1091.6 213.9 %copy-start.38 = (f32[512]{0:T(512)S(1)}, f32[512]{0:T(512)}, u32[]{:S(2)}) copy-start(f32[512]{0:T(512)} %copy-done.37) | copy-start | bytes 6148
  1305.4 209.9 %copy-start.36 = (f32[512]{0:T(512)S(1)}, f32[512]{0:T(512)}, u32[]{:S(2)}) copy-start(f32[512]{0:T(512)} %copy-done.35) | copy-start | bytes 6148
  1512.0 3.4 copy-start.4
  1515.4 2.6 copy-start.11
  1518.1 1.6 copy-start.14
  1521.9 1.3 copy-start.16
  1521.9 1.6 copy-start.18
  1523.5 1.4 copy-start.13
  1523.5 1.5 copy-start.27
  1523.5 1.7 copy-start.30
Sparse Core Ops, SparseCore 0:
  265.9 292.0 reduce-scatter.6
  608.1 208.5 reduce-scatter.8
  823.1 98.5 all-gather.2
  923.6 97.6 all-gather.4
  1045.2 20.2 reduce-scatter.14
  1067.8 22.0 reduce-scatter.16
  1093.5 207.8 reduce-scatter.10
  1305.0 206.9 reduce-scatter.12
